TPU v7x, 128 devices: a whole 4x4x4 slice. The times are simulated.
128 devices in a mesh: dp: 4 (over y), row: 4 (over z_hi, core), col: 8 (over x, z_lo).
Axes of the slice: x: 4, y: 4, z: 4 (z_hi: 2, z_lo: 2; z = z_hi * 2 + z_lo), core: 2. Of those that a mesh axis runs over, the one named last changes fastest.
Arguments:
- latent: bfloat16 [4, 64, 64, 2240], P('dp', 'row', 'col'), may hold values from -40 to 40
- query_weight: bfloat16 [2240, 1120], replicated, may hold values from -0.125 to 0.125
- key_weight: bfloat16 [2240, 1120], replicated, may hold values from -0.125 to 0.125
- value_weight: bfloat16 [2240, 1120], replicated, may hold values from -0.125 to 0.125
- upstream_grad: bfloat16 [4, 64, 64, 1120], P('dp', 'row', 'col'), may hold values from -6 to 6
Outputs:
- latent_grad: bfloat16 [4, 64, 64, 2240], P('dp', 'row', 'col')
- query_weight_grad: float32 [2240, 1120], P(('row', 'col'), 'dp')
- key_weight_grad: float32 [2240, 1120], P(('row', 'col'), 'dp')
- value_weight_grad: float32 [2240, 1120], P(('row', 'col'), 'dp')
All inputs are finite; a program needn't handle non-finite values.
Results may differ from a plain program's by a relative error of at most 0.039.
Values sent between devices are 32-bit elements; how exact they have to be, the bound alone decides.
No kernel may reach another device: no remote copies, remote signals or barrier semaphores. Data moves between devices by JAX's collectives and lax.ppermute only.
A program may use at most 192 MiB of HBM per device.

v0:
```python
import math
import jax
import jax.numpy as jnp
from jax import lax
from jax.sharding import PartitionSpec as P

D = 2240
HD = 112
HEADS = 10
EPSILON = 1e-15
HIGHEST_PRECISION = lax.Precision.HIGHEST


def project(token_rows, weight):
    return jnp.dot(token_rows, weight, preferred_element_type=jnp.float32).astype(jnp.bfloat16)


def back_project(gradient, weight):
    return lax.dot_general(
        gradient, weight, (((1,), (1,)), ((), ())), preferred_element_type=jnp.float32
    )


def body(latent, query_weight, key_weight, value_weight, upstream_grad):
    grid_devices = lax.axis_size("row") * lax.axis_size("col")
    replicas = lax.axis_size("dp")
    token_rows = latent.reshape(-1, D)
    local_count = token_rows.shape[0]
    image_tokens = local_count * grid_devices
    loss_scale = 4.0 * math.sqrt(image_tokens)
    normalizer = 1.0 / math.sqrt(image_tokens * replicas)
    head_width = HEADS * HD
    key_rows = project(token_rows, key_weight)
    value_rows = project(token_rows, value_weight)
    relu_key = jax.nn.relu(key_rows).reshape(-1, HEADS, HD)
    value_heads = value_rows.reshape(-1, HEADS, HD)
    local_state = jnp.einsum(
        "thj,thm->hjm", relu_key, value_heads, preferred_element_type=jnp.float32
    )
    local_total = jnp.sum(relu_key, axis=0, dtype=jnp.float32)
    key_state, key_total = lax.psum((local_state, local_total), ("row", "col"))
    query_rows = project(token_rows, query_weight)
    query_heads = query_rows.reshape(-1, HEADS, HD)
    relu_query = jax.nn.relu(query_heads)
    denominator = (
        jnp.einsum(
            "thj,hj->th",
            relu_query,
            key_total,
            precision=HIGHEST_PRECISION,
            preferred_element_type=jnp.float32,
        )
        + EPSILON
    )
    attended = (
        jnp.einsum(
            "thj,hjm->thm",
            relu_query,
            key_state,
            precision=HIGHEST_PRECISION,
            preferred_element_type=jnp.float32,
        )
        / denominator[:, :, None]
    )
    cotangent = upstream_grad.reshape(-1, HEADS, HD).astype(jnp.float32) * loss_scale
    grad_numer = cotangent / denominator[:, :, None]
    grad_denom = -jnp.sum(cotangent * attended, axis=2) / denominator
    grad_numer_low = grad_numer.astype(jnp.bfloat16)
    local_state_grad = jnp.einsum(
        "thj,thm->hjm", relu_query, grad_numer_low, preferred_element_type=jnp.float32
    )
    local_total_grad = jnp.einsum(
        "thj,th->hj",
        relu_query,
        grad_denom,
        precision=HIGHEST_PRECISION,
        preferred_element_type=jnp.float32,
    )
    state_grad, total_grad = lax.psum((local_state_grad, local_total_grad), ("row", "col"))
    grad_relu_query = (
        jnp.einsum(
            "thm,hjm->thj",
            grad_numer_low,
            key_state,
            precision=HIGHEST_PRECISION,
            preferred_element_type=jnp.float32,
        )
        + grad_denom[:, :, None] * key_total[None]
    )
    grad_query = (
        jnp.where(query_heads > 0, grad_relu_query, 0.0)
        .reshape(-1, head_width)
        .astype(jnp.bfloat16)
    )
    grad_value = (
        jnp.einsum(
            "thj,hjm->thm",
            relu_key,
            state_grad,
            precision=HIGHEST_PRECISION,
            preferred_element_type=jnp.float32,
        )
        .reshape(-1, head_width)
        .astype(jnp.bfloat16)
    )
    grad_relu_key = (
        jnp.einsum(
            "thm,hjm->thj",
            value_heads,
            state_grad,
            precision=HIGHEST_PRECISION,
            preferred_element_type=jnp.float32,
        )
        + total_grad[None]
    )
    grad_key = (
        jnp.where(key_rows.reshape(-1, HEADS, HD) > 0, grad_relu_key, 0.0)
        .reshape(-1, head_width)
        .astype(jnp.bfloat16)
    )
    summed = back_project(grad_query, query_weight) + back_project(grad_key, key_weight)
    summed = summed + back_project(grad_value, value_weight)
    latent_grad = summed.astype(jnp.bfloat16).reshape(latent.shape)
    stacked = jnp.stack([grad_query, grad_key, grad_value], axis=1).reshape(
        local_count, 3, replicas, head_width // replicas
    )
    stacked = jnp.transpose(stacked, (0, 2, 1, 3)).reshape(local_count, 3 * head_width)
    row_block = lax.psum_scatter(
        lax.dot_general(
            token_rows, stacked, (((0,), (0,)), ((), ())), preferred_element_type=jnp.float32
        )
        * normalizer,
        ("row", "col"),
        scatter_dimension=0,
        tiled=True,
    )
    weight_block = lax.psum_scatter(row_block, "dp", scatter_dimension=1, tiled=True)
    weight_block = weight_block.reshape(weight_block.shape[0], 3, head_width // replicas)
    return (latent_grad, weight_block[:, 0], weight_block[:, 1], weight_block[:, 2])


def solution(mesh):
    return jax.shard_map(
        body,
        mesh=mesh,
        in_specs=(P("dp", "row", "col", None), P(), P(), P(), P("dp", "row", "col", None)),
        out_specs=(
            P("dp", "row", "col", None),
            P(("row", "col"), "dp"),
            P(("row", "col"), "dp"),
            P(("row", "col"), "dp"),
        ),
        check_vma=False,
    )
```

profile of v0, /device:TPU:1, one launch (start us, length us, event | category | flops | bytes accessed | tf_op | source)
XLA Modules:
  0.0 548.4 jit_solution(5383486594765757244)
XLA Ops:
  7.2 1.0 copy-done
  8.2 4.7 broadcast_compare_fusion.1
  13.0 4.6 broadcast_maximum_fusion.1
  17.6 2.2 convolution_convert_fusion
  19.9 0.6 mul.36
  20.5 0.3 copy.27
  20.8 0.2 convert_reduce_fusion
  21.1 62.9 %psum.29 = f32[10,112]{1,0:T(8,128)S(1)} all-reduce(f32[10,112]{1,0:T(8,128)S(1)} %reduce_sum.21), channel_id=1, replica_groups=mesh['dp'=4,'row'=4,'col'=8] {'row','col'}, use_global_device_ids=true, to_apply=%region_2.3 | all-reduce | flops 1120 | bytes 8960 | tf_op jit(solution)/shard_map/psum | solution.py:41
  84.0 0.3 fusion.17
  84.4 1.1 fusion.21
  85.5 1.2 fusion.19
  86.8 109.0 %all-reduce.8.cloned.1.call-done = (f32[10,112,112]{2,1,0:T(8,128)}, f32[10,112,112]{2,1,0:T(8,128)}) async-done(((f32[10,112,112]{2,1,0:T(8,128)}, f32[10,112,112]{2,1,0:T(8,128)}), (f32[10,112,112]{2,1,0:T(8,128)}, f32[10,112,112]{2,1,0:T(8,128)})) %all-reduce.8.cloned.1.call-update) | async-done | bytes 1003536 | tf_op jit(solution)/shard_map/psum | solution.py:41
  195.8 1.8 fusion.9
  197.6 1.6 fusion.8
  199.2 0.5 fusion.15
  199.7 59.9 %psum.31 = f32[10,112]{1,0:T(8,128)S(1)} all-reduce(f32[10,112]{1,0:T(8,128)S(1)} %bitcast.132), channel_id=1, replica_groups=mesh['dp'=4,'row'=4,'col'=8] {'row','col'}, use_global_device_ids=true, to_apply=%region_5.6 | all-reduce | flops 1120 | bytes 8960 | tf_op jit(solution)/shard_map/psum | solution.py:79
  259.7 0.6 convolution_convert_fusion.3
  260.3 0.5 fusion.7
  260.9 12.2 %multiply_bitcast_fusion = f32[2240,3360]{0,1:T(8,128)} fusion(bf16[128,3360]{0,1:T(8,128)(2,1)S(1)} %bitcast.110, bf16[1,16,8,2240]{3,2,1,0:T(8,128)(2,1)S(1)} %copy-done), kind=kOutput, calls=%fused_computation | convolution fusion | flops 1934284800 | bytes 31539200 | tf_op jit(solution)/shard_map/dot_general | solution.py:129
  273.2 0.6 copy-done.5
  273.7 0.6 dynamic-slice
  275.0 232.8 %all-reduce.6.cloned.1.call-done = f32[2240,3360]{0,1:T(8,128)} async-done(((f32[2240,3360]{0,1:T(8,128)}), f32[2240,3360]{0,1:T(8,128)}) %all-reduce.6.cloned.1.call-update) | async-done | bytes 30105616
  507.8 3.7 constant_dynamic-slice_fusion
  511.5 4.1 fusion.22
  515.7 4.1 convolution_add_fusion.1
  519.9 1.6 fusion
  521.4 1.1 copy.31
  522.5 16.0 %reduce-scatter.5.cloned.1.call-done = f32[70,840]{0,1:T(8,128)} async-done(((f32[70,3360]{0,1:T(8,128)}), f32[70,840]{0,1:T(8,128)}) %reduce-scatter.5.cloned.1.call-update) | async-done | bytes 235216
  538.5 1.1 fusion.20
  539.5 0.8 copy.46
  540.3 0.8 copy.47
  541.1 0.8 copy.48
  (29 shorter events, 0.5 us)
Async XLA Ops:
  7.2 1.1 copy-start
  7.2 188.6 %all-reduce.8.cloned.1.call-start = ((), (), s32[]{:S(2)}) async-start(), calls=%async_computation.3 | async-start | bytes 2293760 | tf_op jit(solution)/shard_map/psum | solution.py:41
  8.2 9.4 %copy-start.2 = (bf16[2240,1120]{1,0:T(8,128)(2,1)S(1)}, bf16[2240,1120]{1,0:T(8,128)(2,1)}, u32[]{:S(2)}) copy-start(bf16[2240,1120]{1,0:T(8,128)(2,1)} %param.8) | copy-start | bytes 15052804
  13.0 6.9 %copy-start.4 = (bf16[1,16,8,1120]{3,2,1,0:T(8,128)(2,1)S(1)}, bf16[1,16,8,1120]{3,2,1,0:T(8,128)(2,1)}, u32[]{:S(2)}) copy-start(bf16[1,16,8,1120]{3,2,1,0:T(8,128)(2,1)} %param.9) | copy-start | bytes 860164
  86.7 421.1 %all-reduce.6.cloned.1.call-start = ((), (), s32[]{:S(2)}) async-start(), calls=%async_computation.1 | async-start | bytes 61931520
  195.8 63.8 %copy-start.3 = (f32[10,112,112]{2,1,0:T(8,128)S(1)}, f32[10,112,112]{2,1,0:T(8,128)}, u32[]{:S(2)}) copy-start(f32[10,112,112]{2,1,0:T(8,128)} %get-tuple-element.9) | copy-start | bytes 1505284
  273.1 0.7 copy-start.5
  273.1 265.3 %reduce-scatter.5.cloned.1.call-start = ((), (), s32[]{:S(2)}) async-start(), calls=%async_computation.2 | async-start | bytes 2150400
  511.5 8.3 %slice-start = ((s8[5160960]{0:T(1024)(128)(4,1)}), s8[4194304]{0:T(1024)(128)(4,1)S(1)}, s32[]{:S(2)}) async-start(s8[5160960]{0:T(1024)(128)(4,1)} %bitcast.108), calls=%async_computation.4 | async-start | bytes 8388608
  515.7 4.2 slice-start.1
  519.8 22.0 %copy-start.1 = (bf16[1,16,8,2240]{3,2,1,0:T(8,128)(2,1)S(1)}, bf16[1,16,8,2240]{3,2,1,0:T(8,128)(2,1)}, u32[]{:S(2)}) copy-start(bf16[1,16,8,2240]{3,2,1,0:T(8,128)(2,1)} %param.5) | copy-start | bytes 1720324
Sparse Core Ops, SparseCore 0:
  86.8 108.9 all-reduce.7
  273.2 234.5 all-reduce.5
  511.6 26.7 reduce-scatter.4
where the time goes:
time: 549 us; the launch traced here: 548 us
  waiting for transfers between devices  358 us (65%)
  blocking collectives  123 us (22%)
  matrix products  41.2 us (8%)
  between operations  14.6 us (3%)
  local copies, waits for them, and re-layouts  11.3 us (2%)
    unnamed x5, waiting for transfers between devices  249 us
    psum x1, waiting for transfers between devices, body(): key_state, key_total = lax.psum((local_state, local_total), ('row', 'col'))  109 us
    psum x1, blocking collectives, body(): key_state, key_total = lax.psum((local_state, local_total), ('row', 'col'))  62.9 us
    psum x1, blocking collectives, body(): lax.psum((local_state_grad, local_total_grad), ('row', 'col'))  59.9 us
    dot_general x1, matrix products, body(): lax.dot_general(token_rows, stacked, (((0,), (0,)), ((), ())), preferred_...  12.2 us
    dot_general x3, matrix products, project(): jnp.dot(token_rows, weight, preferred_element_type=jnp.float32)  11.6 us
  transfers between devices with their start and end apart: 3, of which 3 were waited for; matrix products, arithmetic and copies ran while one was open for 2% of the time, Pallas kernels for 0%

commit v1 on v0

--- a/solution.py
+++ b/solution.py
@@ -76,7 +76,7 @@
         precision=HIGHEST_PRECISION,
         preferred_element_type=jnp.float32,
     )
-    state_grad, total_grad = lax.psum((local_state_grad, local_total_grad), ("row", "col"))
+    state_grad, total_grad = lax.psum(lax.psum((local_state_grad, local_total_grad), "row"), "col")
     grad_relu_query = (
         jnp.einsum(
             "thm,hjm->thj",

time: 549 us -> 531 us (0.967)
  blocking collectives: 123 us -> 86 us
  waiting for transfers between devices: 358 us -> 375 us
    psum x0 -> x2, waiting for transfers between devices: none -> 89.6 us  [the longest x1 45.9 us: body(): lax.psum(lax.psum((local_state_grad, local_total_grad), 'row'), 'col')]
    psum x1, waiting for transfers between devices: 109 us -> 35.2 us  [body(): key_state, key_total = lax.psum((local_state, local_total), ('row', 'col'))]
    psum x1 -> x2, blocking collectives: 59.9 us -> 23 us  [the longest x1 16.2 us: body(): lax.psum(lax.psum((local_state_grad, local_total_grad), 'row'), 'col')]
    unnamed x5 -> x7, waiting for transfers between devices: 249 us -> 250 us
  transfers between devices with their start and end apart: 3 -> 5, of which waited for: 3 -> 5; matrix products, arithmetic and copies ran while one was open for 2% -> 4% of each run, Pallas kernels for 0% -> 0%
where the time goes in v1:
time: 531 us
  waiting for transfers between devices  375 us (71%)
  blocking collectives  86 us (16%)
  matrix products  43.2 us (8%)
  between operations  14.7 us (3%)
  local copies, waits for them, and re-layouts  11.3 us (2%)
    unnamed x7, waiting for transfers between devices  250 us
    psum x1, blocking collectives, body(): key_state, key_total = lax.psum((local_state, local_total), ('row', 'col'))  63 us
    psum x1, waiting for transfers between devices, body(): lax.psum(lax.psum((local_state_grad, local_total_grad), 'row'), 'col')  45.9 us
    psum x1, waiting for transfers between devices, body(): lax.psum((local_state_grad, local_total_grad), 'row')  43.7 us
    psum x1, waiting for transfers between devices, body(): key_state, key_total = lax.psum((local_state, local_total), ('row', 'col'))  35.2 us
    psum x1, blocking collectives, body(): lax.psum(lax.psum((local_state_grad, local_total_grad), 'row'), 'col')  16.2 us
    dot_general x1, matrix products, body(): lax.dot_general(token_rows, stacked, (((0,), (0,)), ((), ())), preferred_...  12.2 us
    dot_general x3, matrix products, project(): jnp.dot(token_rows, weight, preferred_element_type=jnp.float32)  11.5 us
  transfers between devices with their start and end apart: 5, of which 5 were waited for; matrix products, arithmetic and copies ran while one was open for 4% of the time, Pallas kernels for 0%

profile of v1, /device:TPU:1, one launch (start us, length us, event | category | flops | bytes accessed | tf_op | source)
XLA Modules:
  0.0 530.6 jit_solution(56521412094113392)
XLA Ops:
  7.2 1.0 copy-done
  8.2 4.7 broadcast_maximum_fusion.1
  13.0 2.1 convolution_convert_fusion
  15.1 1.1 fusion.21
  16.3 4.6 broadcast_compare_fusion.1
  21.2 63.0 %psum.43 = f32[10,112]{1,0:T(8,128)S(1)} all-reduce(f32[10,112]{1,0:T(8,128)S(1)} %reduce_sum.21), channel_id=1, replica_groups=mesh['dp'=4,'row'=4,'col'=8] {'row','col'}, use_global_device_ids=true, to_apply=%region_2.3 | all-reduce | flops 1120 | bytes 8960 | tf_op jit(solution)/shard_map/psum | solution.py:41
  84.2 0.6 mul.36
  85.5 1.2 fusion.19
  86.8 35.2 %all-reduce.7.cloned.1.call-done = f32[10,112,112]{2,1,0:T(8,128)} async-done(((f32[10,112,112]{2,1,0:T(8,128)}), f32[10,112,112]{2,1,0:T(8,128)}) %all-reduce.7.cloned.1.call-update) | async-done | bytes 501776 | tf_op jit(solution)/shard_map/psum | solution.py:41
  122.0 1.7 fusion.9
  123.7 43.7 %all-reduce.9.cloned.1.call-done = f32[10,112,112]{2,1,0:T(8,128)} async-done(((f32[10,112,112]{2,1,0:T(8,128)}), f32[10,112,112]{2,1,0:T(8,128)}) %all-reduce.9.cloned.1.call-update) | async-done | bytes 501776 | tf_op jit(solution)/shard_map/psum | solution.py:79
  167.5 0.5 fusion.15
  168.0 6.7 %psum.46 = f32[10,112]{1,0:T(8,128)S(1)} all-reduce(f32[10,112]{1,0:T(8,128)S(1)} %bitcast.132), channel_id=1, replica_groups=mesh['dp'=4,'row'=4,'col'=8] {'row'}, use_global_device_ids=true, to_apply=%region_6.7 | all-reduce | flops 1120 | bytes 8960 | tf_op jit(solution)/shard_map/psum | solution.py:79
  174.8 16.2 %psum.47 = f32[10,112]{1,0:T(8,128)S(1)} all-reduce(f32[10,112]{1,0:T(8,128)S(1)} %psum.46), channel_id=1, replica_groups=mesh['dp'=4,'row'=4,'col'=8] {'col'}, use_global_device_ids=true, to_apply=%region_7.8 | all-reduce | flops 1120 | bytes 8960 | tf_op jit(solution)/shard_map/psum | solution.py:79
  191.0 1.6 fusion.8
  192.6 45.9 %all-reduce.11.cloned.1.call-done = f32[10,112,112]{2,1,0:T(8,128)} async-done(((f32[10,112,112]{2,1,0:T(8,128)}), f32[10,112,112]{2,1,0:T(8,128)}) %all-reduce.11.cloned.1.call-update) | async-done | bytes 501776 | tf_op jit(solution)/shard_map/psum | solution.py:79
  238.5 1.7 convolution_convert_fusion.3
  240.2 1.5 fusion.7
  241.8 12.2 %multiply_bitcast_fusion = f32[2240,3360]{0,1:T(8,128)} fusion(bf16[128,3360]{0,1:T(8,128)(2,1)S(1)} %bitcast.110, bf16[1,16,8,2240]{3,2,1,0:T(8,128)(2,1)S(1)} %copy-done), kind=kOutput, calls=%fused_computation | convolution fusion | flops 1934284800 | bytes 31539200 | tf_op jit(solution)/shard_map/dot_general | solution.py:129
  254.1 0.6 copy-done.4
  254.7 0.6 dynamic-slice
  255.9 234.1 %all-reduce.13.cloned.1.call-done = f32[2240,3360]{0,1:T(8,128)} async-done(((f32[2240,3360]{0,1:T(8,128)}), f32[2240,3360]{0,1:T(8,128)}) %all-reduce.13.cloned.1.call-update) | async-done | bytes 30105616
  490.0 3.7 constant_dynamic-slice_fusion
  493.7 4.1 fusion.22
  497.9 4.1 convolution_add_fusion.1
  502.1 1.6 fusion
  503.6 1.1 copy.31
  504.7 15.9 %reduce-scatter.5.cloned.1.call-done = f32[70,840]{0,1:T(8,128)} async-done(((f32[70,3360]{0,1:T(8,128)}), f32[70,840]{0,1:T(8,128)}) %reduce-scatter.5.cloned.1.call-update) | async-done | bytes 235216
  520.6 1.1 fusion.20
  521.7 0.8 copy.46
  522.5 0.8 copy.47
  523.3 0.8 copy.48
  (34 shorter events, 1.5 us)
Async XLA Ops:
  7.2 1.1 copy-start
  7.2 114.8 %all-reduce.7.cloned.1.call-start = ((), (), s32[]{:S(2)}) async-start(), calls=%async_computation.1 | async-start | bytes 1146880 | tf_op jit(solution)/shard_map/psum | solution.py:41
  8.2 4.7 copy-start.2
  15.1 69.0 %copy-start.3 = (bf16[1,16,8,1120]{3,2,1,0:T(8,128)(2,1)S(1)}, bf16[1,16,8,1120]{3,2,1,0:T(8,128)(2,1)}, u32[]{:S(2)}) copy-start(bf16[1,16,8,1120]{3,2,1,0:T(8,128)(2,1)} %param.9) | copy-start | bytes 860164
  16.3 151.1 %all-reduce.9.cloned.1.call-start = ((), (), s32[]{:S(2)}) async-start(), calls=%async_computation.2 | async-start | bytes 1146880 | tf_op jit(solution)/shard_map/psum | solution.py:79
  86.7 151.8 %all-reduce.11.cloned.1.call-start = ((), (), s32[]{:S(2)}) async-start(), calls=%async_computation.3 | async-start | bytes 1146880 | tf_op jit(solution)/shard_map/psum | solution.py:79
  167.4 322.6 %all-reduce.13.cloned.1.call-start = ((), (), s32[]{:S(2)}) async-start(), calls=%async_computation.4 | async-start | bytes 61931520
  254.0 0.7 copy-start.4
  254.1 266.6 %reduce-scatter.5.cloned.1.call-start = ((), (), s32[]{:S(2)}) async-start(), calls=%async_computation.5 | async-start | bytes 2150400
  493.7 8.3 %slice-start = ((s8[5160960]{0:T(1024)(128)(4,1)}), s8[4194304]{0:T(1024)(128)(4,1)S(1)}, s32[]{:S(2)}) async-start(s8[5160960]{0:T(1024)(128)(4,1)} %bitcast.108), calls=%async_computation.6 | async-start | bytes 8388608
  497.9 4.2 slice-start.1
  502.0 22.0 %copy-start.1 = (bf16[1,16,8,2240]{3,2,1,0:T(8,128)(2,1)S(1)}, bf16[1,16,8,2240]{3,2,1,0:T(8,128)(2,1)}, u32[]{:S(2)}) copy-start(bf16[1,16,8,2240]{3,2,1,0:T(8,128)(2,1)} %param.5) | copy-start | bytes 1720324
Sparse Core Ops, SparseCore 0:
  16.4 105.5 all-reduce.6
  124.5 42.8 all-reduce.8
  169.9 68.5 all-reduce.10
  254.2 235.7 all-reduce.12
  493.8 26.7 reduce-scatter.4
